TPU v7x, 256 devices: a whole 4x4x8 slice. The times are simulated.
256 devices in a mesh: track: 16 (over z, x_lo), tm: 16 (over x_hi, y, core).
Axes of the slice: x: 4 (x_hi: 2, x_lo: 2; x = x_hi * 2 + x_lo), y: 4, z: 8, core: 2. Of those that a mesh axis runs over, the one named last changes fastest.
Arguments:
- positions: float32 [3, 32, 6144], P(None, 'tm', 'track'), may hold values from -6 to 6
- embeddings: float32 [32, 128, 6144], P('tm', None, 'track'), may hold values from -6 to 6
- visible: int32 [32, 6144], P('tm', 'track'), may hold values 0 or 1
Outputs:
- grad_positions: float32 [3, 32, 6144], P(None, 'tm', 'track')
- grad_embeddings: float32 [32, 128, 6144], P('tm', None, 'track')
- mean_loss: float32 [], replicated
All inputs are finite; a program needn't handle non-finite values. No bound on the sum of `visible` on one device may be relied on, other than what follows from the above.
Results may differ from a plain program's by a relative error of at most 0.00014.
Values sent between devices are 32-bit elements; how exact they have to be, the bound alone decides.
A program may use at most 128 MiB of HBM per device.

v0:
```python
import math
import jax
import jax.numpy as jnp
from jax import lax
from jax.sharding import PartitionSpec as P

rigidity = 4.0
highest = lax.Precision.HIGHEST


def shifted(array, axis, by):
    size = lax.axis_size(axis)
    pairs = [(i, i + by) for i in range(size) if 0 <= i + by < size]
    return lax.ppermute(array, axis, pairs)


def tile_terms(pos_a, mask_a, emb_a, pos_b, mask_b, emb_b, weight_scale):
    inv_root = 1.0 / math.sqrt(emb_a.shape[1])
    offset = pos_a[:, :, :, None] - pos_b[:, :, None, :]
    distance = jnp.sqrt(jnp.sum(offset * offset, axis=0) + 1.0)
    change = distance[1:] - distance[:-1]
    both_seen = mask_a[:, :, None] * mask_b[:, None, :]
    seen_pair = both_seen[1:] * both_seen[:-1]
    logits = jnp.einsum("fei,fej->fij", emb_a, emb_b, precision=highest) * inv_root
    affinity = jax.nn.sigmoid(logits)
    squared = seen_pair * change * change
    energy = jnp.sum(affinity * squared)
    grad_change = 2.0 * weight_scale * affinity * seen_pair * change
    padding = jnp.zeros_like(grad_change[:1])
    grad_dist = jnp.concatenate([padding, grad_change], 0) - jnp.concatenate(
        [grad_change, padding], 0
    )
    scaled = (grad_dist / distance)[None] * offset
    grad_pos_a = jnp.sum(scaled, axis=3)
    grad_pos_b = -jnp.sum(scaled, axis=2)
    grad_logit = weight_scale * squared * affinity * (1.0 - affinity) * inv_root
    grad_emb_a = jnp.einsum("fij,fej->fei", grad_logit, emb_b, precision=highest)
    grad_emb_b = jnp.einsum("fij,fei->fej", grad_logit, emb_a, precision=highest)
    return (energy, grad_pos_a, grad_emb_a, grad_pos_b, grad_emb_b)


def on_device(positions, embeddings, visible):
    frames_local = embeddings.shape[0]
    block_width = embeddings.shape[2]
    tracks = block_width * lax.axis_size("track")
    frames = frames_local * lax.axis_size("tm")
    weight_scale = rigidity / math.sqrt(tracks)
    seen_mask = visible.astype(jnp.float32)
    next_pos, next_mask = shifted((positions[:, :1], seen_mask[:1]), "tm", -1)
    pos_ext = jnp.concatenate([positions, next_pos], 1)
    mask_ext = jnp.concatenate([seen_mask, next_mask], 0)
    packed = jnp.concatenate([pos_ext, mask_ext[None]], 0)

    def own_tile(others_packed, others_emb):
        return tile_terms(
            pos_ext,
            mask_ext,
            embeddings,
            others_packed[:3],
            others_packed[3],
            others_emb,
            weight_scale,
        )

    initial = (jnp.zeros_like(pos_ext), jnp.zeros_like(embeddings), jnp.zeros((), jnp.float32))
    piece_packed = lax.all_gather(packed, "track", axis=2, tiled=True)
    piece_emb = lax.all_gather(embeddings, "track", axis=2, tiled=True)
    columns = piece_emb.shape[2]
    blocks = columns // block_width
    split_packed = jnp.moveaxis(
        piece_packed.reshape(4, frames_local + 1, blocks, block_width), 2, 0
    )
    split_emb = jnp.moveaxis(
        piece_emb.reshape(frames_local, piece_emb.shape[1], blocks, block_width), 2, 0
    )

    def advance(inner, others):
        energy, grad_pos_a, grad_emb_a, unused_pos, unused_emb = own_tile(others[0], others[1])
        return ((inner[0] + grad_pos_a, inner[1] + grad_emb_a, inner[2] + energy), None)

    result, unused = lax.scan(advance, initial, (split_packed, split_emb))
    grad_pos, grad_emb, energy_sum = result
    energy_sum = 0.5 * energy_sum
    incoming = shifted(grad_pos[:, -1:], "tm", 1)
    grad_positions = grad_pos[:, :-1]
    grad_positions = jnp.concatenate([grad_positions[:, :1] + incoming, grad_positions[:, 1:]], 1)
    total = lax.psum(energy_sum, ("track", "tm"))
    mean_loss = total / (tracks * (tracks - 1) / 2.0 * (frames - 1))
    return (grad_positions, grad_emb, mean_loss)


def solution(mesh):
    in_specs = (P(None, "tm", "track"), P("tm", None, "track"), P("tm", "track"))
    out_specs = (P(None, "tm", "track"), P("tm", None, "track"), P())
    return jax.shard_map(
        on_device, mesh=mesh, in_specs=in_specs, out_specs=out_specs, check_vma=False
    )
```

profile of v0, /device:TPU:1, one launch (start us, length us, event | category | flops | bytes accessed | tf_op | source)
XLA Modules:
  0.0 581.3 jit_solution(791380038999158030)
XLA Ops:
  7.2 1.9 copy.30
  9.9 5.1 collective-permute-start
  15.7 1.9 collective-permute-start.1
  17.6 3.0 collective-permute-done.1
  21.3 41.1 %all_gather.7 = f32[4,3,6144]{2,1,0:T(4,128)S(1)} all-gather(f32[4,3,384]{2,1,0:T(4,128)S(1)} %pad_maximum_fusion), channel_id=1, replica_groups=mesh['track'=16,'tm'=16] {'track'}, dimensions={2}, use_global_device_ids=true | all-gather | bytes 313344 | tf_op jit(solution)/shard_map/all_gather | solution.py:66
  63.9 97.0 %all-gather.2.cloned.1.call-done = f32[2,128,6144]{1,2,0:T(8,128)} async-done(((f32[2,128,384]{1,2,0:T(8,128)}), f32[2,128,6144]{1,2,0:T(8,128)}) %all-gather.2.cloned.1.call-update) | async-done | bytes 6291472 | tf_op jit(solution)/shard_map/all_gather | solution.py:67
  160.9 327.7 %while.15 = (s32[]{:T(128)}, f32[3,3,384]{2,1,0:T(4,128)}, f32[2,128,384]{2,1,0:T(8,128)}, f32[]{:T(128)}, f32[16,2,128,384]{2,3,0,1:T(8,128)}, /*index=5*/f32[2...) while((s32[]{:T(128)}, f32[3,3,384]{2,1,0:T(4,128)}, ...), condition=%wide.region_4.5_spmd.clone, body=%wide.region_0.4_spmd.clone.sunk | while | flops 922389888 | bytes 49315164 | solution.py:81
  167.0 5.0 multiply_reduce_fusion.2
  172.7 4.3 convolution_add_fusion.2
  187.4 5.0 multiply_reduce_fusion.2
  193.2 4.4 convolution_add_fusion.2
  207.9 5.0 multiply_reduce_fusion.2
  213.6 4.4 convolution_add_fusion.2
  219.9 1.8 fusion.35
  228.4 5.0 multiply_reduce_fusion.2
  234.1 4.4 convolution_add_fusion.2
  248.9 5.0 multiply_reduce_fusion.2
  254.6 4.4 convolution_add_fusion.2
  260.9 1.8 fusion.35
  269.4 5.0 multiply_reduce_fusion.2
  275.1 4.4 convolution_add_fusion.2
  281.3 1.8 fusion.35
  289.9 5.0 multiply_reduce_fusion.2
  295.6 4.4 convolution_add_fusion.2
  310.3 5.0 multiply_reduce_fusion.2
  316.1 4.4 convolution_add_fusion.2
  322.3 1.8 fusion.35
  330.8 5.0 multiply_reduce_fusion.2
  336.6 4.4 convolution_add_fusion.2
  351.3 5.0 multiply_reduce_fusion.2
  357.1 4.4 convolution_add_fusion.2
  363.3 1.8 fusion.35
  371.8 5.0 multiply_reduce_fusion.2
  377.5 4.4 convolution_add_fusion.2
  383.8 1.8 fusion.35
  392.3 5.0 multiply_reduce_fusion.2
  398.0 4.4 convolution_add_fusion.2
  404.3 1.8 fusion.35
  412.8 5.0 multiply_reduce_fusion.2
  418.5 4.4 convolution_add_fusion.2
  433.3 5.0 multiply_reduce_fusion.2
  439.0 4.4 convolution_add_fusion.2
  453.7 5.0 multiply_reduce_fusion.2
  459.5 4.4 convolution_add_fusion.2
  474.2 5.0 multiply_reduce_fusion.2
  480.0 4.4 convolution_add_fusion.2
  489.4 4.8 collective-permute-start.2
  494.2 77.0 %psum.7 = f32[]{:T(128)} all-reduce(f32[]{:T(128)S(6)} %mul_shard_map.3), channel_id=1, replica_groups=mesh['track'=16,'tm'=16] {'track','tm'}, use_global_device_ids=true, to_apply=%region_5.6 | all-reduce | flops 1 | bytes 8 | tf_op jit(solution)/shard_map/psum | solution.py:87
  (379 shorter events, 157.2 us)
Async XLA Ops:
  7.2 56.1 %copy-start.6 = (f32[3,2,384]{2,1,0:T(2,128)S(1)}, f32[3,2,384]{2,1,0:T(2,128)}, u32[]{:S(2)}) copy-start(f32[3,2,384]{2,1,0:T(2,128)} %param.5) | copy-start | bytes 27652
  7.2 153.8 %all-gather.2.cloned.1.call-start = ((), (), s32[]{:S(2)}) async-start(), calls=%async_computation | async-start | bytes 6684672 | tf_op jit(solution)/shard_map/all_gather | solution.py:67
  9.9 7.7 %collective-permute-start = (f32[1,384]{1,0:T(1,128)S(1)}, f32[1,384]{1,0:T(1,128)S(1)}, u32[]{:S(2)}, u32[]{:S(2)}) collective-permute-start(f32[1,384]{1,0:T(1,128)S(1)} %slice.53), channel_id=1, source_target_pairs={{1,0},{2,1},{3,2},{4,3},{5,4},{6,5},{7,6},{8,7},{9,8},{10,9},{11,1... | collective-permute-start | bytes 4616 | tf_op jit(solution)/shard_map/ppermute | solution.py:14
  15.7 4.9 collective-permute-start.1
  166.7 5.4 copy-start
  172.7 4.3 copy-start.1
  178.9 1.8 copy-start.3
  187.1 5.4 copy-start
  193.1 4.4 copy-start.1
  207.6 5.4 copy-start
  213.6 4.4 copy-start.1
  219.9 1.8 copy-start.3
  228.0 5.4 copy-start
  234.1 4.4 copy-start.1
  248.5 5.4 copy-start
  254.6 4.4 copy-start.1
  260.8 1.8 copy-start.3
  269.0 5.4 copy-start
  275.1 4.4 copy-start.1
  281.3 1.8 copy-start.3
  289.5 5.4 copy-start
  295.6 4.4 copy-start.1
  301.8 1.8 copy-start.3
  310.0 5.4 copy-start
  316.1 4.4 copy-start.1
  322.3 1.8 copy-start.3
  330.5 5.4 copy-start
  336.6 4.4 copy-start.1
  342.8 1.8 copy-start.3
  351.0 5.4 copy-start
  357.0 4.4 copy-start.1
  363.3 1.8 copy-start.3
  371.4 5.4 copy-start
  377.5 4.4 copy-start.1
  383.8 1.8 copy-start.3
  391.9 5.4 copy-start
  398.0 4.4 copy-start.1
  404.3 1.8 copy-start.3
  412.4 5.4 copy-start
  418.5 4.4 copy-start.1
  432.9 5.4 copy-start
  439.0 4.4 copy-start.1
  445.2 1.8 copy-start.3
  453.4 5.4 copy-start
  459.5 4.4 copy-start.1
  473.9 5.4 copy-start
  480.0 4.4 copy-start.1
  489.4 82.5 %collective-permute-start.2 = (f32[3,1,384]{2,1,0:T(1,128)S(1)}, f32[3,1,384]{2,1,0:T(1,128)S(1)}, u32[]{:S(2)}, u32[]{:S(2)}) collective-permute-start(f32[3,1,384]{2,1,0:T(1,128)S(1)} %slice.41), channel_id=1, source_target_pairs={{0,1},{1,2},{2,3},{3,4},{4,5},{5,6},{6,7},{7,8},{8,9},{9,10},{10,1... | collective-permute-start | bytes 13832 | tf_op jit(solution)/shard_map/ppermute | solution.py:14
  (53 other events, 44.3 us)
Sparse Core Ops, SparseCore 0:
  9.8 151.1 all-gather.1
where the time goes:
time: 586 us; the launch traced here: 581 us
  matrix products  151 us (26%)
  blocking collectives  118 us (20%)
  waiting for transfers between devices  100 us (17%)
  local copies, waits for them, and re-layouts  94.3 us (16%)
  other arithmetic  77.4 us (13%)
  between operations  15.9 us (3%)
  loops' own time  12.7 us (2%)
  starting transfers between devices  11.9 us (2%)
    all_gather x1, waiting for transfers between devices, on_device(): piece_emb = lax.all_gather(embeddings, 'track', axis=2, tiled=True)  97 us
    dot_general x16, matrix products, tile_terms(): jnp.einsum('fei,fej->fij', emb_a, emb_b, precision=highest) * inv_root  80.6 us
    psum x1, blocking collectives, on_device(): total = lax.psum(energy_sum, ('track', 'tm'))  77 us
    dot_general x16, matrix products, tile_terms(): jnp.einsum('fij,fej->fei', grad_logit, emb_b, precision=highest)  70.5 us
    all_gather x1, blocking collectives, on_device(): piece_packed = lax.all_gather(packed, 'track', axis=2, tiled=True)  41.1 us
    reduce_sum x16, other arithmetic, tile_terms(): grad_pos_a = jnp.sum(scaled, axis=3)  28.8 us
    while x224, local copies, waits for them, and re-layouts  24.9 us
    reduce_sum x16, other arithmetic, tile_terms(): distance = jnp.sqrt(jnp.sum(offset * offset, axis=0) + 1.0)  24.9 us
  transfers between devices with their start and end apart: 4, of which 2 were waited for; matrix products, arithmetic and copies ran while one was open for 1% of the time, Pallas kernels for 0%

commit v1 on v0

--- a/solution.py
+++ b/solution.py
@@ -6,6 +6,12 @@
 
 rigidity = 4.0
 highest = lax.Precision.HIGHEST
+
+
+def _supply_row(array_in):
+    for q in ("track", "tm"):
+        array_in = lax.psum(array_in, axis_name=q)
+    return array_in
 
 
 def shifted(array, axis, by):
@@ -84,7 +90,7 @@
     incoming = shifted(grad_pos[:, -1:], "tm", 1)
     grad_positions = grad_pos[:, :-1]
     grad_positions = jnp.concatenate([grad_positions[:, :1] + incoming, grad_positions[:, 1:]], 1)
-    total = lax.psum(energy_sum, ("track", "tm"))
+    total = _supply_row(energy_sum)
     mean_loss = total / (tracks * (tracks - 1) / 2.0 * (frames - 1))
     return (grad_positions, grad_emb, mean_loss)
 

time: 586 us -> 572 us (0.976)
  blocking collectives: 118 us -> 106 us
    psum x1 -> x2, blocking collectives: 77 us -> 65.2 us  [_supply_row(): array_in = lax.psum(array_in, axis_name=q)]
where the time goes in v1:
time: 572 us; the launch traced here: 567 us
  matrix products  150 us (26%)
  blocking collectives  106 us (19%)
  waiting for transfers between devices  101 us (18%)
  local copies, waits for them, and re-layouts  94.2 us (16%)
  other arithmetic  77.4 us (14%)
  between operations  15.9 us (3%)
  starting transfers between devices  11.4 us (2%)
  loops' own time  10.9 us (2%)
    all_gather x1, waiting for transfers between devices, on_device(): piece_emb = lax.all_gather(embeddings, 'track', axis=2, tiled=True)  98.2 us
    dot_general x16, matrix products, tile_terms(): jnp.einsum('fei,fej->fij', emb_a, emb_b, precision=highest) * inv_root  79.7 us
    dot_general x16, matrix products, tile_terms(): jnp.einsum('fij,fej->fei', grad_logit, emb_b, precision=highest)  70.5 us
    psum x2, blocking collectives, _supply_row(): array_in = lax.psum(array_in, axis_name=q)  65.2 us
    all_gather x1, blocking collectives, on_device(): piece_packed = lax.all_gather(packed, 'track', axis=2, tiled=True)  40.4 us
    reduce_sum x16, other arithmetic, tile_terms(): grad_pos_a = jnp.sum(scaled, axis=3)  28.8 us
    reduce_sum x16, other arithmetic, tile_terms(): distance = jnp.sqrt(jnp.sum(offset * offset, axis=0) + 1.0)  24.9 us
    while x224, local copies, waits for them, and re-layouts  24.9 us
  transfers between devices with their start and end apart: 4, of which 2 were waited for; matrix products, arithmetic and copies ran while one was open for 1% of the time, Pallas kernels for 0%

profile of v1, /device:TPU:1, one launch (start us, length us, event | category | flops | bytes accessed | tf_op | source)
XLA Modules:
  0.0 566.7 jit_solution(10009080141768730305)
XLA Ops:
  7.2 1.9 copy.30
  9.8 5.1 collective-permute-start
  15.7 1.9 collective-permute-start.1
  17.6 3.0 collective-permute-done.1
  21.3 40.4 %all_gather.7 = f32[4,3,6144]{2,1,0:T(4,128)S(1)} all-gather(f32[4,3,384]{2,1,0:T(4,128)S(1)} %pad_maximum_fusion), channel_id=1, replica_groups=mesh['track'=16,'tm'=16] {'track'}, dimensions={2}, use_global_device_ids=true | all-gather | bytes 313344 | tf_op jit(solution)/shard_map/all_gather | solution.py:72
  63.3 98.2 %all-gather.2.cloned.1.call-done = f32[2,128,6144]{1,2,0:T(8,128)} async-done(((f32[2,128,384]{1,2,0:T(8,128)}), f32[2,128,6144]{1,2,0:T(8,128)}) %all-gather.2.cloned.1.call-update) | async-done | bytes 6291472 | tf_op jit(solution)/shard_map/all_gather | solution.py:73
  161.5 324.9 %while.15 = (s32[]{:T(128)}, f32[3,3,384]{2,1,0:T(4,128)}, f32[2,128,384]{2,1,0:T(8,128)}, f32[]{:T(128)}, f32[16,2,128,384]{2,3,0,1:T(8,128)}, /*index=5*/f32[2...) while((s32[]{:T(128)}, f32[3,3,384]{2,1,0:T(4,128)}, ...), condition=%wide.region_4.5_spmd.clone, body=%wide.region_0.4_spmd.clone.sunk | while | flops 922389888 | bytes 49315164 | solution.py:87
  167.5 5.0 multiply_reduce_fusion.2
  173.1 4.3 convolution_add_fusion.2
  187.8 5.0 multiply_reduce_fusion.2
  193.3 4.4 convolution_add_fusion.2
  199.6 1.8 fusion.35
  208.1 5.0 multiply_reduce_fusion.2
  213.6 4.4 convolution_add_fusion.2
  219.9 1.8 fusion.35
  228.4 5.0 multiply_reduce_fusion.2
  233.9 4.4 convolution_add_fusion.2
  240.2 1.8 fusion.35
  248.7 5.0 multiply_reduce_fusion.2
  254.3 4.4 convolution_add_fusion.2
  260.5 1.8 fusion.35
  269.0 5.0 multiply_reduce_fusion.2
  274.6 4.4 convolution_add_fusion.2
  280.8 1.8 fusion.35
  289.3 5.0 multiply_reduce_fusion.2
  294.9 4.4 convolution_add_fusion.2
  301.1 1.8 fusion.35
  309.6 5.0 multiply_reduce_fusion.2
  315.2 4.4 convolution_add_fusion.2
  329.9 5.0 multiply_reduce_fusion.2
  335.5 4.4 convolution_add_fusion.2
  350.3 5.0 multiply_reduce_fusion.2
  355.8 4.4 convolution_add_fusion.2
  370.6 5.0 multiply_reduce_fusion.2
  376.1 4.4 convolution_add_fusion.2
  390.9 5.0 multiply_reduce_fusion.2
  396.4 4.4 convolution_add_fusion.2
  411.2 5.0 multiply_reduce_fusion.2
  416.8 4.4 convolution_add_fusion.2
  431.5 5.0 multiply_reduce_fusion.2
  437.1 4.4 convolution_add_fusion.2
  451.8 5.0 multiply_reduce_fusion.2
  457.4 4.4 convolution_add_fusion.2
  472.1 5.0 multiply_reduce_fusion.2
  477.7 4.4 convolution_add_fusion.2
  487.1 4.3 collective-permute-start.2
  491.4 26.6 %psum.14 = f32[]{:T(128)} all-reduce(f32[]{:T(128)S(6)} %mul_shard_map.3), channel_id=1, replica_groups=mesh['track'=16,'tm'=16] {'track'}, use_global_device_ids=true, to_apply=%region_5.6 | all-reduce | flops 1 | bytes 8 | tf_op jit(solution)/shard_map/psum | solution.py:13
  518.1 38.5 %psum.15 = f32[]{:T(128)} all-reduce(f32[]{:T(128)} %psum.14), channel_id=1, replica_groups=mesh['track'=16,'tm'=16] {'tm'}, use_global_device_ids=true, to_apply=%region_6.7 | all-reduce | flops 1 | bytes 8 | tf_op jit(solution)/shard_map/psum | solution.py:13
  (380 shorter events, 158.9 us)
Async XLA Ops:
  7.2 55.5 %copy-start.6 = (f32[3,2,384]{2,1,0:T(2,128)S(1)}, f32[3,2,384]{2,1,0:T(2,128)}, u32[]{:S(2)}) copy-start(f32[3,2,384]{2,1,0:T(2,128)} %param.5) | copy-start | bytes 27652
  7.2 154.3 %all-gather.2.cloned.1.call-start = ((), (), s32[]{:S(2)}) async-start(), calls=%async_computation | async-start | bytes 6684672 | tf_op jit(solution)/shard_map/all_gather | solution.py:73
  9.8 7.7 %collective-permute-start = (f32[1,384]{1,0:T(1,128)S(1)}, f32[1,384]{1,0:T(1,128)S(1)}, u32[]{:S(2)}, u32[]{:S(2)}) collective-permute-start(f32[1,384]{1,0:T(1,128)S(1)} %slice.53), channel_id=1, source_target_pairs={{1,0},{2,1},{3,2},{4,3},{5,4},{6,5},{7,6},{8,7},{9,8},{10,9},{11,1... | collective-permute-start | bytes 4616 | tf_op jit(solution)/shard_map/ppermute | solution.py:20
  15.7 4.9 collective-permute-start.1
  167.2 5.3 copy-start
  173.1 4.3 copy-start.1
  187.4 5.3 copy-start
  193.3 4.4 copy-start.1
  199.6 1.8 copy-start.3
  207.7 5.3 copy-start
  213.6 4.4 copy-start.1
  219.9 1.8 copy-start.3
  228.0 5.3 copy-start
  233.9 4.4 copy-start.1
  240.2 1.8 copy-start.3
  248.3 5.3 copy-start
  254.3 4.4 copy-start.1
  260.5 1.8 copy-start.3
  268.7 5.3 copy-start
  274.6 4.4 copy-start.1
  280.8 1.8 copy-start.3
  289.0 5.3 copy-start
  294.9 4.4 copy-start.1
  301.1 1.8 copy-start.3
  309.3 5.3 copy-start
  315.2 4.4 copy-start.1
  321.4 1.8 copy-start.3
  329.6 5.3 copy-start
  335.5 4.4 copy-start.1
  341.7 1.8 copy-start.3
  349.9 5.3 copy-start
  355.8 4.4 copy-start.1
  362.1 1.8 copy-start.3
  370.2 5.3 copy-start
  376.1 4.4 copy-start.1
  382.4 1.8 copy-start.3
  390.5 5.3 copy-start
  396.4 4.4 copy-start.1
  402.7 1.8 copy-start.3
  410.8 5.3 copy-start
  416.7 4.4 copy-start.1
  431.1 5.3 copy-start
  437.1 4.4 copy-start.1
  451.5 5.3 copy-start
  457.4 4.4 copy-start.1
  471.8 5.3 copy-start
  477.7 4.4 copy-start.1
  487.1 70.2 %collective-permute-start.2 = (f32[3,1,384]{2,1,0:T(1,128)S(1)}, f32[3,1,384]{2,1,0:T(1,128)S(1)}, u32[]{:S(2)}, u32[]{:S(2)}) collective-permute-start(f32[3,1,384]{2,1,0:T(1,128)S(1)} %slice.41), channel_id=1, source_target_pairs={{0,1},{1,2},{2,3},{3,4},{4,5},{5,6},{6,7},{7,8},{8,9},{9,10},{10,1... | collective-permute-start | bytes 13832 | tf_op jit(solution)/shard_map/ppermute | solution.py:20
  (53 other events, 44.2 us)
Sparse Core Ops, SparseCore 0:
  9.8 151.6 all-gather.1
